TPU v7x, 256 devices: a whole 4x4x8 slice. The times are simulated.
256 devices in a mesh: gx: 16 (over z, core), gy: 16 (over y, x).
Axes of the slice: x: 4, y: 4, z: 8, core: 2. Of those that a mesh axis runs over, the one named last changes fastest.
Arguments:
- populations: float32 [19, 8, 128, 2048], P(None, None, 'gy', 'gx'), may hold values from 0.49 to 22.2, as said below
- concentrations: float32 [3, 8, 128, 2048], P(None, None, 'gy', 'gx'), may hold values from 0.5 to 2
- potential: float32 [8, 128, 2048], P(None, 'gy', 'gx'), may hold values from -5 to 5
- solid_mask: int32 [8, 128, 2048], P(None, 'gy', 'gx'), may hold values 0 or 1
- surface_sign: int32 [8, 128, 2048], P(None, 'gy', 'gx'), may hold values from -1 to 1
Outputs:
- populations_new: float32 [19, 8, 128, 2048], P(None, None, 'gy', 'gx')
- concentrations_new: float32 [3, 8, 128, 2048], P(None, None, 'gy', 'gx')
- potential_new: float32 [8, 128, 2048], P(None, 'gy', 'gx')
Inputs may be any that keep to these rules, and one draw needn't show every extreme that they name: `populations`: every entry is positive, near 36 times the weight of its velocity times a density of order one. `solid_mask`: 1 marks a solid cell, 0 a fluid one. `surface_sign`: read only at solid cells.
All inputs are finite; a program needn't handle non-finite values. No bound on the sum of `solid_mask` on one device may be relied on, other than what follows from the above.
Results may differ from a plain program's by a relative error of at most 0.0018.
Values sent between devices are 32-bit elements; how exact they have to be, the bound alone decides.
No kernel may reach another device: no remote copies, remote signals or barrier semaphores. Data moves between devices by JAX's collectives and lax.ppermute only.
A program may use at most 64 MiB of HBM per device.

v0:
```python
import jax
import jax.numpy as jnp
import numpy as np
from jax import lax
from jax.sharding import PartitionSpec as P

STEPS = 4
CYCLES = 2
SSTEP = 4
lattice_velocity = (
    (0, 0, 0),
    (0, 0, 1),
    (0, 0, -1),
    (0, 1, 0),
    (0, -1, 0),
    (1, 0, 0),
    (-1, 0, 0),
    (0, 1, 1),
    (0, -1, -1),
    (0, 1, -1),
    (0, -1, 1),
    (1, 0, 1),
    (-1, 0, -1),
    (1, 0, -1),
    (-1, 0, 1),
    (1, 1, 0),
    (-1, -1, 0),
    (1, -1, 0),
    (-1, 1, 0),
)
opposite = (0, 2, 1, 4, 3, 6, 5, 8, 7, 10, 9, 12, 11, 14, 13, 16, 15, 18, 17)
lattice_weight = (1.0 / 3.0,) + (1.0 / 18.0,) * 6 + (1.0 / 36.0,) * 12
moving = (1, 2, 3, 4, 7, 8, 9, 10, 11, 12, 13, 14, 15, 16, 17, 18)
relax_time = 1.25
force_scale = 0.05
valences = (1.0, -1.0, 2.0)
diffusivity = (0.05, 0.07, 0.03)
diag_coef = 6.0001
surface_scale = 2.0


def padded_2(block, sides, width):
    for axis, dim in sides:
        count = lax.axis_size(axis)
        forward = [(i, i + 1) for i in range(count - 1)]
        forward.append((count - 1, 0))
        backward = [(target, source) for source, target in forward]
        low = lax.ppermute(
            lax.slice_in_dim(block, block.shape[dim] - width, None, axis=dim), axis, forward
        )
        high = lax.ppermute(lax.slice_in_dim(block, 0, width, axis=dim), axis, backward)
        block = jnp.concatenate([low, block, high], axis=dim)
    return block


def lattice_dot(direction, vector):
    running = None
    for axis_id in range(3):
        if direction[axis_id] != 0:
            addend = vector[axis_id] if direction[axis_id] > 0 else -vector[axis_id]
            running = addend if running is None else running + addend
    return running


def ion_charge(concentration):
    return (
        valences[0] * concentration[0]
        + valences[1] * concentration[1]
        + valences[2] * concentration[2]
    )


def collide_cells(fields, concentration, fluid_mask, efield):
    density = fields[0]
    for member in range(1, 19):
        density = density + fields[member]
    momentum = []
    for axis_id in range(3):
        running = None
        for member in range(19):
            sign_val = lattice_velocity[member][axis_id]
            if sign_val != 0:
                addend = fields[member] if sign_val > 0 else -fields[member]
                running = addend if running is None else running + addend
        momentum.append(running)
    charge = fluid_mask * ion_charge(concentration)
    forcing = [force_scale * charge * efield[axis_id] for axis_id in range(3)]
    velocity = [(momentum[axis_id] + 0.5 * forcing[axis_id]) / density for axis_id in range(3)]
    speed_sq = velocity[0] * velocity[0] + velocity[1] * velocity[1] + velocity[2] * velocity[2]
    work_rate = velocity[0] * forcing[0] + velocity[1] * forcing[1] + velocity[2] * forcing[2]
    relaxed = []
    for member in range(19):
        weight = lattice_weight[member]
        if member == 0:
            projected = jnp.zeros_like(density)
            along_force = jnp.zeros_like(density)
        else:
            projected = lattice_dot(lattice_velocity[member], velocity)
            along_force = lattice_dot(lattice_velocity[member], forcing)
        balance = (
            weight
            * density
            * (1.0 + 3.0 * projected + 4.5 * projected * projected - 1.5 * speed_sq)
        )
        source = weight * (3.0 * (along_force - work_rate) + 9.0 * projected * along_force)
        relaxed.append(
            fields[member]
            - (fields[member] - balance) / relax_time
            + (1.0 - 0.5 / relax_time) * source
        )
    return (relaxed, velocity)


def face_flux(low, high, pot_low, pot_high, vel_low, vel_high, opened):
    rates = jnp.array(diffusivity, jnp.float32).reshape(3, 1, 1, 1)
    drift = jnp.array(valences, jnp.float32).reshape(3, 1, 1, 1) * rates
    middle = 0.5 * (low + high)
    return opened * (
        -rates * (high - low)
        - drift * middle * (pot_high - pot_low)
        + 0.5 * (vel_low + vel_high) * middle
    )


def ion_step(concentration, velocity, potential, fluid_mask, ion_pad, pot_rim, fluid_rim):
    fluxes = face_flux(
        concentration,
        jnp.roll(concentration, -1, 1),
        potential,
        jnp.roll(potential, -1, 0),
        velocity[0],
        jnp.roll(velocity[0], -1, 0),
        fluid_mask * jnp.roll(fluid_mask, -1, 0),
    )
    running = fluxes - jnp.roll(fluxes, 1, 1)
    conc_in = ion_pad[:3, :, :, 1:-1]
    pot_in = pot_rim[:, :, 1:-1]
    vel_in = ion_pad[3, :, :, 1:-1]
    open_in = fluid_rim[:, :, 1:-1]
    fluxes = face_flux(
        conc_in[:, :, :-1],
        conc_in[:, :, 1:],
        pot_in[:, :-1],
        pot_in[:, 1:],
        vel_in[:, :-1],
        vel_in[:, 1:],
        open_in[:, :-1] * open_in[:, 1:],
    )
    running = running + (fluxes[:, :, 1:] - fluxes[:, :, :-1])
    conc_in = ion_pad[:3, :, 1:-1, :]
    pot_in = pot_rim[:, 1:-1, :]
    vel_in = ion_pad[4, :, 1:-1, :]
    open_in = fluid_rim[:, 1:-1, :]
    fluxes = face_flux(
        conc_in[..., :-1],
        conc_in[..., 1:],
        pot_in[..., :-1],
        pot_in[..., 1:],
        vel_in[..., :-1],
        vel_in[..., 1:],
        open_in[..., :-1] * open_in[..., 1:],
    )
    running = running + (fluxes[..., 1:] - fluxes[..., :-1])
    return concentration - running


def neighbor_sum(padded):
    core = padded[:, :, 1:-1, 1:-1]
    return (
        jnp.roll(core, -1, 1)
        + jnp.roll(core, 1, 1)
        + (padded[:, :, 2:, 1:-1] + padded[:, :, :-2, 1:-1])
        + (padded[:, :, 1:-1, 2:] + padded[:, :, 1:-1, :-2])
    )


def next_level(summed, previous):
    if previous is None:
        return -summed / 6.0
    return -summed / 3.0 - previous


def shift_table():
    order_m = 2 * SSTEP + 1
    coeffs = np.zeros((order_m, order_m), np.float32)
    for block_start in (0, SSTEP + 1):
        block_depth = SSTEP if block_start == 0 else SSTEP - 1
        for column in range(block_depth):
            coeffs[block_start + column, block_start + column] = diag_coef
            coeffs[block_start + column + 1, block_start + column] = 6.0 if column == 0 else 3.0
            if column > 0:
                coeffs[block_start + column - 1, block_start + column] = 3.0
    return coeffs


def krylov_steps(gram_matrix):
    order_m = 2 * SSTEP + 1
    highest = lax.Precision.HIGHEST
    coeffs = jnp.asarray(shift_table(), jnp.float32)
    search_co = jnp.zeros((order_m,), jnp.float32).at[0].set(1.0)
    resid_co = jnp.zeros((order_m,), jnp.float32).at[SSTEP + 1].set(1.0)
    sol_co = jnp.zeros((order_m,), jnp.float32)
    residual_sq = jnp.dot(
        resid_co, jnp.dot(gram_matrix, resid_co, precision=highest), precision=highest
    )
    for inner_id in range(SSTEP):
        image_co = jnp.dot(coeffs, search_co, precision=highest)
        step_len = residual_sq / jnp.dot(
            search_co, jnp.dot(gram_matrix, image_co, precision=highest), precision=highest
        )
        sol_co = sol_co + step_len * search_co
        resid_co = resid_co - step_len * image_co
        fresh_sq = jnp.dot(
            resid_co, jnp.dot(gram_matrix, resid_co, precision=highest), precision=highest
        )
        search_co = resid_co + fresh_sq / residual_sq * search_co
        residual_sq = fresh_sq
    return (sol_co, resid_co, search_co)


def local(populations, concentrations, potential, solid_mask, surface_sign):
    highest = lax.Precision.HIGHEST
    fluid_mask = 1.0 - solid_mask.astype(jnp.float32)
    rows_y = potential.shape[1]
    cols_x = potential.shape[2]
    rims = padded_2(jnp.stack([potential, fluid_mask]), (("gx", 3), ("gy", 2)), 1)
    pot_rim = rims[0]
    fluid_rim = rims[1]
    efield = [
        (jnp.roll(potential, 1, 0) - jnp.roll(potential, -1, 0)) * 0.5,
        (pot_rim[:, :-2, 1:-1] - pot_rim[:, 2:, 1:-1]) * 0.5,
        (pot_rim[:, 1:-1, :-2] - pot_rim[:, 1:-1, 2:]) * 0.5,
    ]
    source_open = []
    for member in range(19):
        offset = lattice_velocity[member]
        window = fluid_rim[
            :, 1 - offset[1] : 1 - offset[1] + rows_y, 1 - offset[2] : 1 - offset[2] + cols_x
        ]
        source_open.append(jnp.roll(window, offset[0], 0))
    fields = [populations[member] for member in range(19)]
    concentration = concentrations
    for time_step in range(STEPS):
        relaxed, velocity = collide_cells(fields, concentration, fluid_mask, efield)
        stacked = jnp.concatenate(
            [
                jnp.stack([relaxed[member] for member in moving]),
                concentration,
                jnp.stack([velocity[1], velocity[2]]),
            ]
        )
        lattice_pad = padded_2(stacked, (("gx", 3), ("gy", 2)), 1)
        ion_pad = lattice_pad[len(moving) :]
        arrived = []
        for member in range(19):
            offset = lattice_velocity[member]
            if member in moving:
                slot_id = moving.index(member)
                piece = lattice_pad[
                    slot_id,
                    :,
                    1 - offset[1] : 1 - offset[1] + rows_y,
                    1 - offset[2] : 1 - offset[2] + cols_x,
                ]
            else:
                piece = relaxed[member]
            arrived.append(jnp.roll(piece, offset[0], 0))
        updated = [
            jnp.where(
                fluid_mask > 0.5,
                jnp.where(source_open[member] > 0.5, arrived[member], relaxed[opposite[member]]),
                fields[member],
            )
            for member in range(19)
        ]
        concentration = ion_step(
            concentration, velocity, potential, fluid_mask, ion_pad, pot_rim, fluid_rim
        )
        fields = updated
    target = fluid_mask * ion_charge(concentration) + surface_scale * surface_sign.astype(
        jnp.float32
    ) * (1.0 - fluid_mask)
    solution = potential
    start_pad = padded_2(solution[None], (("gx", 3), ("gy", 2)), 1)
    residual = target - (diag_coef * solution - neighbor_sum(start_pad)[0])
    search = residual
    for cycle_id in range(CYCLES):
        p_levels = [search]
        r_levels = [residual]
        previous = None
        current = jnp.stack([search, residual])
        for level_id in range(SSTEP):
            if level_id == SSTEP - 1:
                current = current[:1]
            padded = padded_2(current, (("gx", 3), ("gy", 2)), 1)
            following = next_level(
                neighbor_sum(padded), None if level_id == 0 else previous[: current.shape[0]]
            )
            previous = current
            current = following
            p_levels.append(current[0])
            if current.shape[0] > 1:
                r_levels.append(current[1])
        basis = jnp.stack(p_levels + r_levels)
        local_gram = jnp.einsum("aijk,bijk->ab", basis, basis, precision=highest)
        gram_matrix = lax.psum(local_gram, ("gx", "gy"))
        sol_co, resid_co, search_co = krylov_steps(gram_matrix)
        solution = solution + jnp.tensordot(sol_co, basis, axes=1, precision=highest)
        residual = jnp.tensordot(resid_co, basis, axes=1, precision=highest)
        search = jnp.tensordot(search_co, basis, axes=1, precision=highest)
    return (jnp.stack(fields), concentration, solution)


def solution(mesh):
    placed = (
        P(None, None, "gy", "gx"),
        P(None, None, "gy", "gx"),
        P(None, "gy", "gx"),
        P(None, "gy", "gx"),
        P(None, "gy", "gx"),
    )
    return jax.shard_map(
        local,
        mesh=mesh,
        in_specs=placed,
        out_specs=(P(None, None, "gy", "gx"), P(None, None, "gy", "gx"), P(None, "gy", "gx")),
        check_vma=False,
    )
```

profile of v0, /device:TPU:1, one launch (start us, length us, event | category | flops | bytes accessed | tf_op | source)
XLA Modules:
  0.0 479.0 jit_solution(2040877553520355775)
XLA Ops:
  2.4 3.0 collective-permute-start
  11.4 3.8 collective-permute-start.3
  32.1 3.3 collective-permute-start.5
  43.5 5.4 %collective-permute-start.7 = (f32[21,8,1,130]{3,2,1,0:T(1,128)S(1)}, f32[21,8,1,130]{3,2,1,0:T(1,128)S(1)}, u32[]{:S(2)}, u32[]{:S(2)}) collective-permute-start(f32[21,8,1,130]{3,2,1,0:T(1,128)S(1)} %get-tuple-element.347), channel_id=1, source_target_pairs={{1,0},{2,1},{3,2},{4,3},{5,4},{6,5},{7,6},{8,7},{9,8},{10,9},{11,1... | collective-permute-start | bytes 262088 | tf_op jit(solution)/shard_map/ppermute | solution.py:51
  70.3 3.0 collective-permute-start.9
  79.4 5.8 %collective-permute-start.11 = (f32[21,8,1,130]{3,2,1,0:T(1,128)S(1)}, f32[21,8,1,130]{3,2,1,0:T(1,128)S(1)}, u32[]{:S(2)}, u32[]{:S(2)}) collective-permute-start(f32[21,8,1,130]{3,2,1,0:T(1,128)S(1)} %get-tuple-element.341), channel_id=1, source_target_pairs={{1,0},{2,1},{3,2},{4,3},{5,4},{6,5},{7,6},{8,7},{9,8},{10,9},{11,1... | collective-permute-start | bytes 262088 | tf_op jit(solution)/shard_map/ppermute | solution.py:51
  89.6 2.3 fusion.481
  106.0 3.1 collective-permute-start.13
  115.1 5.6 %collective-permute-start.15 = (f32[21,8,1,130]{3,2,1,0:T(1,128)S(1)}, f32[21,8,1,130]{3,2,1,0:T(1,128)S(1)}, u32[]{:S(2)}, u32[]{:S(2)}) collective-permute-start(f32[21,8,1,130]{3,2,1,0:T(1,128)S(1)} %get-tuple-element.335), channel_id=1, source_target_pairs={{1,0},{2,1},{3,2},{4,3},{5,4},{6,5},{7,6},{8,7},{9,8},{10,9},{11,1... | collective-permute-start | bytes 262088 | tf_op jit(solution)/shard_map/ppermute | solution.py:51
  121.0 2.4 collective-permute-done.14
  125.4 2.3 fusion.600
  141.5 3.2 collective-permute-start.17
  146.2 5.1 %collective-permute-start.22 = (f32[1,8,1,130]{3,2,1,0:T(1,128)}, f32[1,8,1,130]{3,2,1,0:T(1,128)}, u32[]{:S(2)}, u32[]{:S(2)}) collective-permute-start(f32[1,8,1,130]{3,2,1,0:T(1,128)} %get-tuple-element.428), channel_id=1, source_target_pairs={{1,0},{2,1},{3,2},{4,3},{5,4},{6,5},{7,6},{8,7},{9,8},{10,9},{11,1... | collective-permute-start | bytes 12488 | tf_op jit(solution)/shard_map/ppermute | solution.py:51
  156.5 4.8 %collective-permute-start.19 = (f32[21,8,1,130]{3,2,1,0:T(1,128)S(1)}, f32[21,8,1,130]{3,2,1,0:T(1,128)S(1)}, u32[]{:S(2)}, u32[]{:S(2)}) collective-permute-start(f32[21,8,1,130]{3,2,1,0:T(1,128)S(1)} %get-tuple-element.328), channel_id=1, source_target_pairs={{1,0},{2,1},{3,2},{4,3},{5,4},{6,5},{7,6},{8,7},{9,8},{10,9},{11,1... | collective-permute-start | bytes 262088 | tf_op jit(solution)/shard_map/ppermute | solution.py:51
  170.8 3.6 collective-permute-start.25
  184.3 5.2 %collective-permute-start.26 = (f32[2,8,1,130]{3,0,2,1:T(2,128)S(1)}, f32[2,8,1,130]{3,0,2,1:T(2,128)S(1)}, u32[]{:S(2)}, u32[]{:S(2)}) collective-permute-start(f32[2,8,1,130]{3,0,2,1:T(2,128)S(1)} %get-tuple-element.402), channel_id=1, source_target_pairs={{1,0},{2,1},{3,2},{4,3},{5,4},{6,5},{7,6},{8,7},{9,8},{10,9},{11,1... | collective-permute-start | bytes 24968 | tf_op jit(solution)/shard_map/ppermute | solution.py:51
  190.4 5.0 %collective-permute-done.27 = f32[2,8,1,130]{3,0,2,1:T(2,128)S(1)} collective-permute-done((f32[2,8,1,130]{3,0,2,1:T(2,128)S(1)}, f32[2,8,1,130]{3,0,2,1:T(2,128)S(1)}, u32[]{:S(2)}, u32[]{:S(2)}) %collective-permute-start.27) | collective-permute-done | bytes 8352 | tf_op jit(solution)/shard_map/ppermute | solution.py:48
  196.2 4.4 collective-permute-start.29
  204.5 3.1 collective-permute-done.31
  208.2 5.1 %collective-permute-start.33 = (f32[2,8,8,1]{3,0,2,1:T(2,128)S(1)}, f32[2,8,8,1]{3,0,2,1:T(2,128)S(1)}, u32[]{:S(2)}, u32[]{:S(2)}) collective-permute-start(f32[2,8,8,1]{3,0,2,1:T(2,128)S(1)} %get-tuple-element.487), channel_id=1, source_target_pairs={{16,0},{32,16},{48,32},{64,48},{80,64},{96,80},{112,96},{128,112},... | collective-permute-start | bytes 1544 | tf_op jit(solution)/shard_map/ppermute | solution.py:51
  217.4 3.3 collective-permute-done.35
  221.3 5.1 %collective-permute-start.37 = (f32[1,8,8,1]{3,0,2,1:T(1,128)S(1)}, f32[1,8,8,1]{3,0,2,1:T(1,128)S(1)}, u32[]{:S(2)}, u32[]{:S(2)}) collective-permute-start(f32[1,8,8,1]{3,0,2,1:T(1,128)S(1)} %get-tuple-element.481), channel_id=1, source_target_pairs={{16,0},{32,16},{48,32},{64,48},{80,64},{96,80},{112,96},{128,112},... | collective-permute-start | bytes 776 | tf_op jit(solution)/shard_map/ppermute | solution.py:51
  230.3 3.1 collective-permute-done.39
  235.1 78.9 %psum.14 = f32[9,9]{1,0:T(8,128)S(1)} all-reduce(f32[9,9]{1,0:T(8,128)S(1)} %convolution_bitcast_fusion.1), channel_id=1, replica_groups=mesh['gx'=16,'gy'=16] {'gx','gy'}, use_global_device_ids=true, to_apply=%region_0.1 | all-reduce | flops 81 | bytes 648 | tf_op jit(solution)/shard_map/psum | solution.py:306
  335.4 2.3 collective-permute-done.41
  340.5 4.5 collective-permute-done.43
  353.8 3.4 collective-permute-done.47
  358.9 3.0 collective-permute-start.49
  366.1 3.1 collective-permute-done.51
  370.8 4.2 collective-permute-start.53
  378.9 3.1 collective-permute-done.55
  383.7 77.5 %psum.15 = f32[9,9]{1,0:T(8,128)S(1)} all-reduce(f32[9,9]{1,0:T(8,128)S(1)} %convolution_bitcast_fusion), channel_id=1, replica_groups=mesh['gx'=16,'gy'=16] {'gx','gy'}, use_global_device_ids=true, to_apply=%region_1.2 | all-reduce | flops 81 | bytes 648 | tf_op jit(solution)/shard_map/psum | solution.py:306
  (940 shorter events, 182.4 us)
Async XLA Ops:
  2.4 7.5 %collective-permute-start = (f32[2,8,8,1]{3,2,1,0:T(8,128)S(1)}, f32[2,8,8,1]{3,2,1,0:T(8,128)S(1)}, u32[]{:S(2)}, u32[]{:S(2)}) collective-permute-start(f32[2,8,8,1]{3,2,1,0:T(8,128)S(1)} %get-tuple-element.495), channel_id=1, source_target_pairs={{0,16},{16,32},{32,48},{48,64},{64,80},{80,96},{96,112},{112,128},... | collective-permute-start | bytes 1544 | tf_op jit(solution)/shard_map/ppermute | solution.py:48
  6.4 138.3 %collective-permute-start.20 = (f32[1,8,8,1]{3,2,1,0:T(8,128)}, f32[1,8,8,1]{3,2,1,0:T(8,128)}, u32[]{:S(2)}, u32[]{:S(2)}) collective-permute-start(f32[1,8,8,1]{3,2,1,0:T(8,128)} %get-tuple-element.508), channel_id=1, source_target_pairs={{0,16},{16,32},{32,48},{48,64},{64,80},{80,96},{96,112},{112,128},... | collective-permute-start | bytes 776 | tf_op jit(solution)/shard_map/ppermute | solution.py:48
  7.9 136.8 %collective-permute-start.21 = (f32[1,8,8,1]{3,2,1,0:T(8,128)}, f32[1,8,8,1]{3,2,1,0:T(8,128)}, u32[]{:S(2)}, u32[]{:S(2)}) collective-permute-start(f32[1,8,8,1]{3,2,1,0:T(8,128)} %get-tuple-element.507), channel_id=1, source_target_pairs={{16,0},{32,16},{48,32},{64,48},{80,64},{96,80},{112,96},{128,112},... | collective-permute-start | bytes 776 | tf_op jit(solution)/shard_map/ppermute | solution.py:51
  10.1 6.1 %collective-permute-start.2 = (f32[2,8,1,130]{3,2,1,0:T(1,128)S(1)}, f32[2,8,1,130]{3,2,1,0:T(1,128)S(1)}, u32[]{:S(2)}, u32[]{:S(2)}) collective-permute-start(f32[2,8,1,130]{3,2,1,0:T(1,128)S(1)} %get-tuple-element.400), channel_id=1, source_target_pairs={{0,1},{1,2},{2,3},{3,4},{4,5},{5,6},{6,7},{7,8},{8,9},{9,10},{10,1... | collective-permute-start | bytes 24968 | tf_op jit(solution)/shard_map/ppermute | solution.py:48
  30.9 8.9 %collective-permute-start.4 = (f32[21,8,8,1]{0,2,3,1:T(8,128)S(1)}, f32[21,8,8,1]{0,2,3,1:T(8,128)S(1)}, u32[]{:S(2)}, u32[]{:S(2)}) collective-permute-start(f32[21,8,8,1]{0,2,3,1:T(8,128)S(1)} %copy.34), channel_id=1, source_target_pairs={{0,16},{16,32},{32,48},{48,64},{64,80},{80,96},{96,112},{112,128},... | collective-permute-start | bytes 16136 | tf_op jit(solution)/shard_map/ppermute | solution.py:48
  32.1 8.4 %collective-permute-start.5 = (f32[21,8,8,1]{0,2,3,1:T(8,128)S(1)}, f32[21,8,8,1]{0,2,3,1:T(8,128)}, u32[]{:S(2)}, u32[]{:S(2)}) collective-permute-start(f32[21,8,8,1]{0,2,3,1:T(8,128)S(1)} %copy.36), channel_id=1, source_target_pairs={{16,0},{32,16},{48,32},{64,48},{80,64},{96,80},{112,96},{128,112},... | collective-permute-start | bytes 16136 | tf_op jit(solution)/shard_map/ppermute | solution.py:51
  43.4 7.9 %collective-permute-start.6 = (f32[21,8,1,130]{3,2,1,0:T(1,128)S(1)}, f32[21,8,1,130]{3,2,1,0:T(1,128)S(1)}, u32[]{:S(2)}, u32[]{:S(2)}) collective-permute-start(f32[21,8,1,130]{3,2,1,0:T(1,128)S(1)} %get-tuple-element.346), channel_id=1, source_target_pairs={{0,1},{1,2},{2,3},{3,4},{4,5},{5,6},{6,7},{7,8},{8,9},{9,10},{10,1... | collective-permute-start | bytes 262088 | tf_op jit(solution)/shard_map/ppermute | solution.py:48
  43.5 7.8 %collective-permute-start.7 = (f32[21,8,1,130]{3,2,1,0:T(1,128)S(1)}, f32[21,8,1,130]{3,2,1,0:T(1,128)S(1)}, u32[]{:S(2)}, u32[]{:S(2)}) collective-permute-start(f32[21,8,1,130]{3,2,1,0:T(1,128)S(1)} %get-tuple-element.347), channel_id=1, source_target_pairs={{1,0},{2,1},{3,2},{4,3},{5,4},{6,5},{7,6},{8,7},{9,8},{10,9},{11,1... | collective-permute-start | bytes 262088 | tf_op jit(solution)/shard_map/ppermute | solution.py:51
  69.0 7.5 %collective-permute-start.8 = (f32[21,8,8,1]{0,2,3,1:T(8,128)S(1)}, f32[21,8,8,1]{0,2,3,1:T(8,128)S(1)}, u32[]{:S(2)}, u32[]{:S(2)}) collective-permute-start(f32[21,8,8,1]{0,2,3,1:T(8,128)S(1)} %copy.40), channel_id=1, source_target_pairs={{0,16},{16,32},{32,48},{48,64},{64,80},{80,96},{96,112},{112,128},... | collective-permute-start | bytes 16136 | tf_op jit(solution)/shard_map/ppermute | solution.py:48
  70.3 6.9 %collective-permute-start.9 = (f32[21,8,8,1]{0,2,3,1:T(8,128)S(1)}, f32[21,8,8,1]{0,2,3,1:T(8,128)S(1)}, u32[]{:S(2)}, u32[]{:S(2)}) collective-permute-start(f32[21,8,8,1]{0,2,3,1:T(8,128)S(1)} %copy.42), channel_id=1, source_target_pairs={{16,0},{32,16},{48,32},{64,48},{80,64},{96,80},{112,96},{128,112},... | collective-permute-start | bytes 16136 | tf_op jit(solution)/shard_map/ppermute | solution.py:51
  79.4 8.2 %collective-permute-start.10 = (f32[21,8,1,130]{3,2,1,0:T(1,128)S(1)}, f32[21,8,1,130]{3,2,1,0:T(1,128)S(1)}, u32[]{:S(2)}, u32[]{:S(2)}) collective-permute-start(f32[21,8,1,130]{3,2,1,0:T(1,128)S(1)} %get-tuple-element.340), channel_id=1, source_target_pairs={{0,1},{1,2},{2,3},{3,4},{4,5},{5,6},{6,7},{7,8},{8,9},{9,10},{10,1... | collective-permute-start | bytes 262088 | tf_op jit(solution)/shard_map/ppermute | solution.py:48
  79.4 8.2 %collective-permute-start.11 = (f32[21,8,1,130]{3,2,1,0:T(1,128)S(1)}, f32[21,8,1,130]{3,2,1,0:T(1,128)S(1)}, u32[]{:S(2)}, u32[]{:S(2)}) collective-permute-start(f32[21,8,1,130]{3,2,1,0:T(1,128)S(1)} %get-tuple-element.341), channel_id=1, source_target_pairs={{1,0},{2,1},{3,2},{4,3},{5,4},{6,5},{7,6},{8,7},{9,8},{10,9},{11,1... | collective-permute-start | bytes 262088 | tf_op jit(solution)/shard_map/ppermute | solution.py:51
  104.7 7.4 %collective-permute-start.12 = (f32[21,8,8,1]{0,2,3,1:T(8,128)S(1)}, f32[21,8,8,1]{0,2,3,1:T(8,128)S(1)}, u32[]{:S(2)}, u32[]{:S(2)}) collective-permute-start(f32[21,8,8,1]{0,2,3,1:T(8,128)S(1)} %copy.46), channel_id=1, source_target_pairs={{0,16},{16,32},{32,48},{48,64},{64,80},{80,96},{96,112},{112,128},... | collective-permute-start | bytes 16136 | tf_op jit(solution)/shard_map/ppermute | solution.py:48
  106.0 6.9 %collective-permute-start.13 = (f32[21,8,8,1]{0,2,3,1:T(8,128)S(1)}, f32[21,8,8,1]{0,2,3,1:T(8,128)S(1)}, u32[]{:S(2)}, u32[]{:S(2)}) collective-permute-start(f32[21,8,8,1]{0,2,3,1:T(8,128)S(1)} %copy.48), channel_id=1, source_target_pairs={{16,0},{32,16},{48,32},{64,48},{80,64},{96,80},{112,96},{128,112},... | collective-permute-start | bytes 16136 | tf_op jit(solution)/shard_map/ppermute | solution.py:51
  115.0 8.4 %collective-permute-start.14 = (f32[21,8,1,130]{3,2,1,0:T(1,128)S(1)}, f32[21,8,1,130]{3,2,1,0:T(1,128)S(1)}, u32[]{:S(2)}, u32[]{:S(2)}) collective-permute-start(f32[21,8,1,130]{3,2,1,0:T(1,128)S(1)} %get-tuple-element.334), channel_id=1, source_target_pairs={{0,1},{1,2},{2,3},{3,4},{4,5},{5,6},{6,7},{7,8},{8,9},{9,10},{10,1... | collective-permute-start | bytes 262088 | tf_op jit(solution)/shard_map/ppermute | solution.py:48
  115.1 8.3 %collective-permute-start.15 = (f32[21,8,1,130]{3,2,1,0:T(1,128)S(1)}, f32[21,8,1,130]{3,2,1,0:T(1,128)S(1)}, u32[]{:S(2)}, u32[]{:S(2)}) collective-permute-start(f32[21,8,1,130]{3,2,1,0:T(1,128)S(1)} %get-tuple-element.335), channel_id=1, source_target_pairs={{1,0},{2,1},{3,2},{4,3},{5,4},{6,5},{7,6},{8,7},{9,8},{10,9},{11,1... | collective-permute-start | bytes 262088 | tf_op jit(solution)/shard_map/ppermute | solution.py:51
  140.3 13.2 %collective-permute-start.16 = (f32[21,8,8,1]{0,2,3,1:T(8,128)S(1)}, f32[21,8,8,1]{0,2,3,1:T(8,128)S(1)}, u32[]{:S(2)}, u32[]{:S(2)}) collective-permute-start(f32[21,8,8,1]{0,2,3,1:T(8,128)S(1)} %copy.52), channel_id=1, source_target_pairs={{0,16},{16,32},{32,48},{48,64},{64,80},{80,96},{96,112},{112,128},... | collective-permute-start | bytes 16136 | tf_op jit(solution)/shard_map/ppermute | solution.py:48
  141.5 12.8 %collective-permute-start.17 = (f32[21,8,8,1]{0,2,3,1:T(8,128)S(1)}, f32[21,8,8,1]{0,2,3,1:T(8,128)S(1)}, u32[]{:S(2)}, u32[]{:S(2)}) collective-permute-start(f32[21,8,8,1]{0,2,3,1:T(8,128)S(1)} %copy.54), channel_id=1, source_target_pairs={{16,0},{32,16},{48,32},{64,48},{80,64},{96,80},{112,96},{128,112},... | collective-permute-start | bytes 16136 | tf_op jit(solution)/shard_map/ppermute | solution.py:51
  146.2 21.8 %collective-permute-start.22 = (f32[1,8,1,130]{3,2,1,0:T(1,128)}, f32[1,8,1,130]{3,2,1,0:T(1,128)}, u32[]{:S(2)}, u32[]{:S(2)}) collective-permute-start(f32[1,8,1,130]{3,2,1,0:T(1,128)} %get-tuple-element.428), channel_id=1, source_target_pairs={{1,0},{2,1},{3,2},{4,3},{5,4},{6,5},{7,6},{8,7},{9,8},{10,9},{11,1... | collective-permute-start | bytes 12488 | tf_op jit(solution)/shard_map/ppermute | solution.py:51
  151.4 16.7 %collective-permute-start.23 = (f32[1,8,1,130]{3,2,1,0:T(1,128)}, f32[1,8,1,130]{3,2,1,0:T(1,128)}, u32[]{:S(2)}, u32[]{:S(2)}) collective-permute-start(f32[1,8,1,130]{3,2,1,0:T(1,128)} %get-tuple-element.429), channel_id=1, source_target_pairs={{0,1},{1,2},{2,3},{3,4},{4,5},{5,6},{6,7},{7,8},{8,9},{9,10},{10,1... | collective-permute-start | bytes 12488 | tf_op jit(solution)/shard_map/ppermute | solution.py:48
  156.4 7.7 %collective-permute-start.18 = (f32[21,8,1,130]{3,2,1,0:T(1,128)S(1)}, f32[21,8,1,130]{3,2,1,0:T(1,128)S(1)}, u32[]{:S(2)}, u32[]{:S(2)}) collective-permute-start(f32[21,8,1,130]{3,2,1,0:T(1,128)S(1)} %get-tuple-element.329), channel_id=1, source_target_pairs={{0,1},{1,2},{2,3},{3,4},{4,5},{5,6},{6,7},{7,8},{8,9},{9,10},{10,1... | collective-permute-start | bytes 262088 | tf_op jit(solution)/shard_map/ppermute | solution.py:48
  156.5 7.6 %collective-permute-start.19 = (f32[21,8,1,130]{3,2,1,0:T(1,128)S(1)}, f32[21,8,1,130]{3,2,1,0:T(1,128)S(1)}, u32[]{:S(2)}, u32[]{:S(2)}) collective-permute-start(f32[21,8,1,130]{3,2,1,0:T(1,128)S(1)} %get-tuple-element.328), channel_id=1, source_target_pairs={{1,0},{2,1},{3,2},{4,3},{5,4},{6,5},{7,6},{8,7},{9,8},{10,9},{11,1... | collective-permute-start | bytes 262088 | tf_op jit(solution)/shard_map/ppermute | solution.py:51
  170.0 14.1 %collective-permute-start.24 = (f32[2,8,8,1]{3,0,2,1:T(2,128)S(1)}, f32[2,8,8,1]{3,0,2,1:T(2,128)S(1)}, u32[]{:S(2)}, u32[]{:S(2)}) collective-permute-start(f32[2,8,8,1]{3,0,2,1:T(2,128)S(1)} %get-tuple-element.502), channel_id=1, source_target_pairs={{0,16},{16,32},{32,48},{48,64},{64,80},{80,96},{96,112},{112,128},... | collective-permute-start | bytes 1544 | tf_op jit(solution)/shard_map/ppermute | solution.py:48
  170.8 13.4 %collective-permute-start.25 = (f32[2,8,8,1]{3,0,2,1:T(2,128)S(1)}, f32[2,8,8,1]{3,0,2,1:T(2,128)S(1)}, u32[]{:S(2)}, u32[]{:S(2)}) collective-permute-start(f32[2,8,8,1]{3,0,2,1:T(2,128)S(1)} %get-tuple-element.501), channel_id=1, source_target_pairs={{16,0},{32,16},{48,32},{64,48},{80,64},{96,80},{112,96},{128,112},... | collective-permute-start | bytes 1544 | tf_op jit(solution)/shard_map/ppermute | solution.py:51
  184.3 6.1 %collective-permute-start.26 = (f32[2,8,1,130]{3,0,2,1:T(2,128)S(1)}, f32[2,8,1,130]{3,0,2,1:T(2,128)S(1)}, u32[]{:S(2)}, u32[]{:S(2)}) collective-permute-start(f32[2,8,1,130]{3,0,2,1:T(2,128)S(1)} %get-tuple-element.402), channel_id=1, source_target_pairs={{1,0},{2,1},{3,2},{4,3},{5,4},{6,5},{7,6},{8,7},{9,8},{10,9},{11,1... | collective-permute-start | bytes 24968 | tf_op jit(solution)/shard_map/ppermute | solution.py:51
  189.5 5.9 %collective-permute-start.27 = (f32[2,8,1,130]{3,0,2,1:T(2,128)S(1)}, f32[2,8,1,130]{3,0,2,1:T(2,128)S(1)}, u32[]{:S(2)}, u32[]{:S(2)}) collective-permute-start(f32[2,8,1,130]{3,0,2,1:T(2,128)S(1)} %get-tuple-element.403), channel_id=1, source_target_pairs={{0,1},{1,2},{2,3},{3,4},{4,5},{5,6},{6,7},{7,8},{8,9},{9,10},{10,1... | collective-permute-start | bytes 24968 | tf_op jit(solution)/shard_map/ppermute | solution.py:48
  201.7 6.0 %collective-permute-start.31 = (f32[2,8,1,130]{3,0,2,1:T(2,128)S(1)}, f32[2,8,1,130]{3,0,2,1:T(2,128)S(1)}, u32[]{:S(2)}, u32[]{:S(2)}) collective-permute-start(f32[2,8,1,130]{3,0,2,1:T(2,128)S(1)} %get-tuple-element.399), channel_id=1, source_target_pairs={{0,1},{1,2},{2,3},{3,4},{4,5},{5,6},{6,7},{7,8},{8,9},{9,10},{10,1... | collective-permute-start | bytes 24968 | tf_op jit(solution)/shard_map/ppermute | solution.py:48
  208.2 6.0 %collective-permute-start.33 = (f32[2,8,8,1]{3,0,2,1:T(2,128)S(1)}, f32[2,8,8,1]{3,0,2,1:T(2,128)S(1)}, u32[]{:S(2)}, u32[]{:S(2)}) collective-permute-start(f32[2,8,8,1]{3,0,2,1:T(2,128)S(1)} %get-tuple-element.487), channel_id=1, source_target_pairs={{16,0},{32,16},{48,32},{64,48},{80,64},{96,80},{112,96},{128,112},... | collective-permute-start | bytes 1544 | tf_op jit(solution)/shard_map/ppermute | solution.py:51
  214.5 6.2 %collective-permute-start.35 = (f32[2,8,1,130]{3,0,2,1:T(2,128)S(1)}, f32[2,8,1,130]{3,0,2,1:T(2,128)S(1)}, u32[]{:S(2)}, u32[]{:S(2)}) collective-permute-start(f32[2,8,1,130]{3,0,2,1:T(2,128)S(1)} %get-tuple-element.397), channel_id=1, source_target_pairs={{0,1},{1,2},{2,3},{3,4},{4,5},{5,6},{6,7},{7,8},{8,9},{9,10},{10,1... | collective-permute-start | bytes 24968 | tf_op jit(solution)/shard_map/ppermute | solution.py:48
  221.3 6.0 %collective-permute-start.37 = (f32[1,8,8,1]{3,0,2,1:T(1,128)S(1)}, f32[1,8,8,1]{3,0,2,1:T(1,128)S(1)}, u32[]{:S(2)}, u32[]{:S(2)}) collective-permute-start(f32[1,8,8,1]{3,0,2,1:T(1,128)S(1)} %get-tuple-element.481), channel_id=1, source_target_pairs={{16,0},{32,16},{48,32},{64,48},{80,64},{96,80},{112,96},{128,112},... | collective-permute-start | bytes 776 | tf_op jit(solution)/shard_map/ppermute | solution.py:51
  351.2 6.0 %collective-permute-start.47 = (f32[2,8,1,130]{3,0,2,1:T(2,128)S(1)}, f32[2,8,1,130]{3,0,2,1:T(2,128)S(1)}, u32[]{:S(2)}, u32[]{:S(2)}) collective-permute-start(f32[2,8,1,130]{3,0,2,1:T(2,128)S(1)} %get-tuple-element.393), channel_id=1, source_target_pairs={{0,1},{1,2},{2,3},{3,4},{4,5},{5,6},{6,7},{7,8},{8,9},{9,10},{10,1... | collective-permute-start | bytes 24968 | tf_op jit(solution)/shard_map/ppermute | solution.py:48
  363.3 6.0 %collective-permute-start.51 = (f32[2,8,1,130]{3,0,2,1:T(2,128)S(1)}, f32[2,8,1,130]{3,0,2,1:T(2,128)S(1)}, u32[]{:S(2)}, u32[]{:S(2)}) collective-permute-start(f32[2,8,1,130]{3,0,2,1:T(2,128)S(1)} %get-tuple-element.391), channel_id=1, source_target_pairs={{0,1},{1,2},{2,3},{3,4},{4,5},{5,6},{6,7},{7,8},{8,9},{9,10},{10,1... | collective-permute-start | bytes 24968 | tf_op jit(solution)/shard_map/ppermute | solution.py:48
  (299 other events, 792.7 us)
where the time goes:
time: 488 us; the launch traced here: 479 us
  blocking collectives  156 us (32%)
  starting transfers between devices  104 us (21%)
  other arithmetic  70.3 us (14%)
  waiting for transfers between devices  55.8 us (11%)
  local copies, waits for them, and re-layouts  50.7 us (10%)
  between operations  25.1 us (5%)
  matrix products  17.1 us (4%)
    psum x2, blocking collectives, local(): gram_matrix = lax.psum(local_gram, ('gx', 'gy'))  156 us
    ppermute x28, starting transfers between devices, padded_2(): lax.ppermute(lax.slice_in_dim(block, 0, width, axis=dim), axis, backward)  80.6 us
    unnamed x81, other arithmetic  41.9 us
    ppermute x28, waiting for transfers between devices, padded_2(): lax.ppermute(lax.slice_in_dim(block, block.shape[dim] - width, None, axis...  41.5 us
    ppermute x28, starting transfers between devices, padded_2(): lax.ppermute(lax.slice_in_dim(block, block.shape[dim] - width, None, axis...  23 us
    unnamed x538, local copies, waits for them, and re-layouts  22.3 us
    ppermute x28, waiting for transfers between devices, padded_2(): lax.ppermute(lax.slice_in_dim(block, 0, width, axis=dim), axis, backward)  14.2 us
  transfers between devices with their start and end apart: 56, of which 35 were waited for; matrix products, arithmetic and copies ran while one was open for 18% of the time, Pallas kernels for 0%

commit v1 on v0

--- a/solution.py
+++ b/solution.py
@@ -303,7 +303,7 @@
                 r_levels.append(current[1])
         basis = jnp.stack(p_levels + r_levels)
         local_gram = jnp.einsum("aijk,bijk->ab", basis, basis, precision=highest)
-        gram_matrix = lax.psum(local_gram, ("gx", "gy"))
+        gram_matrix = lax.psum(lax.psum(local_gram, "gy"), "gx")
         sol_co, resid_co, search_co = krylov_steps(gram_matrix)
         solution = solution + jnp.tensordot(sol_co, basis, axes=1, precision=highest)
         residual = jnp.tensordot(resid_co, basis, axes=1, precision=highest)

time: 488 us -> 459 us (0.941)
  blocking collectives: 156 us -> 128 us
    psum x2 -> x4, blocking collectives: 156 us -> 128 us  [local(): gram_matrix = lax.psum(lax.psum(local_gram, 'gy'), 'gx')]
  transfers between devices with their start and end apart: 56 -> 56, of which waited for: 35 -> 35; matrix products, arithmetic and copies ran while one was open for 18% -> 20% of each run, Pallas kernels for 0% -> 0%
where the time goes in v1:
time: 459 us; the launch traced here: 450 us
  blocking collectives  128 us (28%)
  starting transfers between devices  104 us (23%)
  other arithmetic  70.3 us (15%)
  waiting for transfers between devices  55.9 us (12%)
  local copies, waits for them, and re-layouts  50.6 us (11%)
  between operations  24.3 us (5%)
  matrix products  16.6 us (4%)
    psum x4, blocking collectives, local(): gram_matrix = lax.psum(lax.psum(local_gram, 'gy'), 'gx')  128 us
    ppermute x28, starting transfers between devices, padded_2(): lax.ppermute(lax.slice_in_dim(block, 0, width, axis=dim), axis, backward)  81.3 us
    ppermute x28, waiting for transfers between devices, padded_2(): lax.ppermute(lax.slice_in_dim(block, block.shape[dim] - width, None, axis...  42.1 us
    unnamed x81, other arithmetic  41.9 us
    ppermute x28, starting transfers between devices, padded_2(): lax.ppermute(lax.slice_in_dim(block, block.shape[dim] - width, None, axis...  22.7 us
    unnamed x538, local copies, waits for them, and re-layouts  22.3 us
    ppermute x28, waiting for transfers between devices, padded_2(): lax.ppermute(lax.slice_in_dim(block, 0, width, axis=dim), axis, backward)  13.8 us
  transfers between devices with their start and end apart: 56, of which 35 were waited for; matrix products, arithmetic and copies ran while one was open for 20% of the time, Pallas kernels for 0%

profile of v1, /device:TPU:1, one launch (start us, length us, event | category | flops | bytes accessed | tf_op | source)
XLA Modules:
  0.0 450.2 jit_solution(2203528703605491214)
XLA Ops:
  2.4 3.0 collective-permute-start
  11.4 3.8 collective-permute-start.3
  32.1 3.3 collective-permute-start.5
  43.5 5.4 %collective-permute-start.7 = (f32[21,8,1,130]{3,2,1,0:T(1,128)S(1)}, f32[21,8,1,130]{3,2,1,0:T(1,128)S(1)}, u32[]{:S(2)}, u32[]{:S(2)}) collective-permute-start(f32[21,8,1,130]{3,2,1,0:T(1,128)S(1)} %get-tuple-element.347), channel_id=1, source_target_pairs={{1,0},{2,1},{3,2},{4,3},{5,4},{6,5},{7,6},{8,7},{9,8},{10,9},{11,1... | collective-permute-start | bytes 262088 | tf_op jit(solution)/shard_map/ppermute | solution.py:51
  70.3 3.0 collective-permute-start.9
  79.4 5.8 %collective-permute-start.11 = (f32[21,8,1,130]{3,2,1,0:T(1,128)S(1)}, f32[21,8,1,130]{3,2,1,0:T(1,128)S(1)}, u32[]{:S(2)}, u32[]{:S(2)}) collective-permute-start(f32[21,8,1,130]{3,2,1,0:T(1,128)S(1)} %get-tuple-element.341), channel_id=1, source_target_pairs={{1,0},{2,1},{3,2},{4,3},{5,4},{6,5},{7,6},{8,7},{9,8},{10,9},{11,1... | collective-permute-start | bytes 262088 | tf_op jit(solution)/shard_map/ppermute | solution.py:51
  89.5 2.3 fusion.481
  106.0 3.1 collective-permute-start.13
  115.1 5.6 %collective-permute-start.15 = (f32[21,8,1,130]{3,2,1,0:T(1,128)S(1)}, f32[21,8,1,130]{3,2,1,0:T(1,128)S(1)}, u32[]{:S(2)}, u32[]{:S(2)}) collective-permute-start(f32[21,8,1,130]{3,2,1,0:T(1,128)S(1)} %get-tuple-element.335), channel_id=1, source_target_pairs={{1,0},{2,1},{3,2},{4,3},{5,4},{6,5},{7,6},{8,7},{9,8},{10,9},{11,1... | collective-permute-start | bytes 262088 | tf_op jit(solution)/shard_map/ppermute | solution.py:51
  121.0 2.4 collective-permute-done.14
  141.4 3.2 collective-permute-start.17
  146.2 5.1 %collective-permute-start.22 = (f32[1,8,1,130]{3,2,1,0:T(1,128)}, f32[1,8,1,130]{3,2,1,0:T(1,128)}, u32[]{:S(2)}, u32[]{:S(2)}) collective-permute-start(f32[1,8,1,130]{3,2,1,0:T(1,128)} %get-tuple-element.428), channel_id=1, source_target_pairs={{1,0},{2,1},{3,2},{4,3},{5,4},{6,5},{7,6},{8,7},{9,8},{10,9},{11,1... | collective-permute-start | bytes 12488 | tf_op jit(solution)/shard_map/ppermute | solution.py:51
  156.5 4.8 %collective-permute-start.19 = (f32[21,8,1,130]{3,2,1,0:T(1,128)S(1)}, f32[21,8,1,130]{3,2,1,0:T(1,128)S(1)}, u32[]{:S(2)}, u32[]{:S(2)}) collective-permute-start(f32[21,8,1,130]{3,2,1,0:T(1,128)S(1)} %get-tuple-element.328), channel_id=1, source_target_pairs={{1,0},{2,1},{3,2},{4,3},{5,4},{6,5},{7,6},{8,7},{9,8},{10,9},{11,1... | collective-permute-start | bytes 262088 | tf_op jit(solution)/shard_map/ppermute | solution.py:51
  170.7 3.6 collective-permute-start.25
  184.2 5.2 %collective-permute-start.26 = (f32[2,8,1,130]{3,0,2,1:T(2,128)S(1)}, f32[2,8,1,130]{3,0,2,1:T(2,128)S(1)}, u32[]{:S(2)}, u32[]{:S(2)}) collective-permute-start(f32[2,8,1,130]{3,0,2,1:T(2,128)S(1)} %get-tuple-element.402), channel_id=1, source_target_pairs={{1,0},{2,1},{3,2},{4,3},{5,4},{6,5},{7,6},{8,7},{9,8},{10,9},{11,1... | collective-permute-start | bytes 24968 | tf_op jit(solution)/shard_map/ppermute | solution.py:51
  190.3 5.0 %collective-permute-done.27 = f32[2,8,1,130]{3,0,2,1:T(2,128)S(1)} collective-permute-done((f32[2,8,1,130]{3,0,2,1:T(2,128)S(1)}, f32[2,8,1,130]{3,0,2,1:T(2,128)S(1)}, u32[]{:S(2)}, u32[]{:S(2)}) %collective-permute-start.27) | collective-permute-done | bytes 8352 | tf_op jit(solution)/shard_map/ppermute | solution.py:48
  196.1 4.4 collective-permute-start.29
  204.5 3.1 collective-permute-done.31
  208.2 5.1 %collective-permute-start.33 = (f32[2,8,8,1]{3,0,2,1:T(2,128)S(1)}, f32[2,8,8,1]{3,0,2,1:T(2,128)S(1)}, u32[]{:S(2)}, u32[]{:S(2)}) collective-permute-start(f32[2,8,8,1]{3,0,2,1:T(2,128)S(1)} %get-tuple-element.487), channel_id=1, source_target_pairs={{16,0},{32,16},{48,32},{64,48},{80,64},{96,80},{112,96},{128,112},... | collective-permute-start | bytes 1544 | tf_op jit(solution)/shard_map/ppermute | solution.py:51
  217.3 3.3 collective-permute-done.35
  221.3 5.1 %collective-permute-start.37 = (f32[1,8,8,1]{3,0,2,1:T(1,128)S(1)}, f32[1,8,8,1]{3,0,2,1:T(1,128)S(1)}, u32[]{:S(2)}, u32[]{:S(2)}) collective-permute-start(f32[1,8,8,1]{3,0,2,1:T(1,128)S(1)} %get-tuple-element.481), channel_id=1, source_target_pairs={{16,0},{32,16},{48,32},{64,48},{80,64},{96,80},{112,96},{128,112},... | collective-permute-start | bytes 776 | tf_op jit(solution)/shard_map/ppermute | solution.py:51
  230.3 3.1 collective-permute-done.39
  235.1 29.3 %psum.28 = f32[9,9]{1,0:T(8,128)S(1)} all-reduce(f32[9,9]{1,0:T(8,128)S(1)} %convolution_bitcast_fusion.1), channel_id=1, replica_groups=mesh['gx'=16,'gy'=16] {'gy'}, use_global_device_ids=true, to_apply=%region_0.1 | all-reduce | flops 81 | bytes 648 | tf_op jit(solution)/shard_map/psum | solution.py:306
  264.4 34.9 %psum.29 = f32[9,9]{1,0:T(8,128)S(1)} all-reduce(f32[9,9]{1,0:T(8,128)S(1)} %psum.28), channel_id=1, replica_groups=mesh['gx'=16,'gy'=16] {'gx'}, use_global_device_ids=true, to_apply=%region_1.2 | all-reduce | flops 81 | bytes 648 | tf_op jit(solution)/shard_map/psum | solution.py:306
  325.4 4.8 %collective-permute-done.43 = f32[2,8,1,130]{3,0,2,1:T(2,128)S(1)} collective-permute-done((f32[2,8,1,130]{3,0,2,1:T(2,128)S(1)}, f32[2,8,1,130]{3,0,2,1:T(2,128)S(1)}, u32[]{:S(2)}, u32[]{:S(2)}) %collective-permute-start.43) | collective-permute-done | bytes 8352 | tf_op jit(solution)/shard_map/ppermute | solution.py:48
  338.8 3.4 collective-permute-done.47
  343.9 3.1 collective-permute-start.49
  351.0 3.4 collective-permute-done.51
  355.9 4.3 collective-permute-start.53
  364.0 3.1 collective-permute-done.55
  368.8 29.4 %psum.30 = f32[9,9]{1,0:T(8,128)S(1)} all-reduce(f32[9,9]{1,0:T(8,128)S(1)} %convolution_bitcast_fusion), channel_id=1, replica_groups=mesh['gx'=16,'gy'=16] {'gy'}, use_global_device_ids=true, to_apply=%region_2.3 | all-reduce | flops 81 | bytes 648 | tf_op jit(solution)/shard_map/psum | solution.py:306
  398.1 34.9 %psum.31 = f32[9,9]{1,0:T(8,128)S(1)} all-reduce(f32[9,9]{1,0:T(8,128)S(1)} %psum.30), channel_id=1, replica_groups=mesh['gx'=16,'gy'=16] {'gx'}, use_global_device_ids=true, to_apply=%region_3.4 | all-reduce | flops 81 | bytes 648 | tf_op jit(solution)/shard_map/psum | solution.py:306
  (942 shorter events, 186.3 us)
Async XLA Ops:
  2.4 7.5 %collective-permute-start = (f32[2,8,8,1]{3,2,1,0:T(8,128)S(1)}, f32[2,8,8,1]{3,2,1,0:T(8,128)S(1)}, u32[]{:S(2)}, u32[]{:S(2)}) collective-permute-start(f32[2,8,8,1]{3,2,1,0:T(8,128)S(1)} %get-tuple-element.495), channel_id=1, source_target_pairs={{0,16},{16,32},{32,48},{48,64},{64,80},{80,96},{96,112},{112,128},... | collective-permute-start | bytes 1544 | tf_op jit(solution)/shard_map/ppermute | solution.py:48
  6.4 138.2 %collective-permute-start.20 = (f32[1,8,8,1]{3,2,1,0:T(8,128)}, f32[1,8,8,1]{3,2,1,0:T(8,128)}, u32[]{:S(2)}, u32[]{:S(2)}) collective-permute-start(f32[1,8,8,1]{3,2,1,0:T(8,128)} %get-tuple-element.508), channel_id=1, source_target_pairs={{0,16},{16,32},{32,48},{48,64},{64,80},{80,96},{96,112},{112,128},... | collective-permute-start | bytes 776 | tf_op jit(solution)/shard_map/ppermute | solution.py:48
  7.9 136.7 %collective-permute-start.21 = (f32[1,8,8,1]{3,2,1,0:T(8,128)}, f32[1,8,8,1]{3,2,1,0:T(8,128)}, u32[]{:S(2)}, u32[]{:S(2)}) collective-permute-start(f32[1,8,8,1]{3,2,1,0:T(8,128)} %get-tuple-element.507), channel_id=1, source_target_pairs={{16,0},{32,16},{48,32},{64,48},{80,64},{96,80},{112,96},{128,112},... | collective-permute-start | bytes 776 | tf_op jit(solution)/shard_map/ppermute | solution.py:51
  10.1 6.1 %collective-permute-start.2 = (f32[2,8,1,130]{3,2,1,0:T(1,128)S(1)}, f32[2,8,1,130]{3,2,1,0:T(1,128)S(1)}, u32[]{:S(2)}, u32[]{:S(2)}) collective-permute-start(f32[2,8,1,130]{3,2,1,0:T(1,128)S(1)} %get-tuple-element.400), channel_id=1, source_target_pairs={{0,1},{1,2},{2,3},{3,4},{4,5},{5,6},{6,7},{7,8},{8,9},{9,10},{10,1... | collective-permute-start | bytes 24968 | tf_op jit(solution)/shard_map/ppermute | solution.py:48
  30.9 8.9 %collective-permute-start.4 = (f32[21,8,8,1]{0,2,3,1:T(8,128)S(1)}, f32[21,8,8,1]{0,2,3,1:T(8,128)S(1)}, u32[]{:S(2)}, u32[]{:S(2)}) collective-permute-start(f32[21,8,8,1]{0,2,3,1:T(8,128)S(1)} %copy.34), channel_id=1, source_target_pairs={{0,16},{16,32},{32,48},{48,64},{64,80},{80,96},{96,112},{112,128},... | collective-permute-start | bytes 16136 | tf_op jit(solution)/shard_map/ppermute | solution.py:48
  32.1 8.4 %collective-permute-start.5 = (f32[21,8,8,1]{0,2,3,1:T(8,128)S(1)}, f32[21,8,8,1]{0,2,3,1:T(8,128)}, u32[]{:S(2)}, u32[]{:S(2)}) collective-permute-start(f32[21,8,8,1]{0,2,3,1:T(8,128)S(1)} %copy.36), channel_id=1, source_target_pairs={{16,0},{32,16},{48,32},{64,48},{80,64},{96,80},{112,96},{128,112},... | collective-permute-start | bytes 16136 | tf_op jit(solution)/shard_map/ppermute | solution.py:51
  43.4 7.9 %collective-permute-start.6 = (f32[21,8,1,130]{3,2,1,0:T(1,128)S(1)}, f32[21,8,1,130]{3,2,1,0:T(1,128)S(1)}, u32[]{:S(2)}, u32[]{:S(2)}) collective-permute-start(f32[21,8,1,130]{3,2,1,0:T(1,128)S(1)} %get-tuple-element.346), channel_id=1, source_target_pairs={{0,1},{1,2},{2,3},{3,4},{4,5},{5,6},{6,7},{7,8},{8,9},{9,10},{10,1... | collective-permute-start | bytes 262088 | tf_op jit(solution)/shard_map/ppermute | solution.py:48
  43.5 7.8 %collective-permute-start.7 = (f32[21,8,1,130]{3,2,1,0:T(1,128)S(1)}, f32[21,8,1,130]{3,2,1,0:T(1,128)S(1)}, u32[]{:S(2)}, u32[]{:S(2)}) collective-permute-start(f32[21,8,1,130]{3,2,1,0:T(1,128)S(1)} %get-tuple-element.347), channel_id=1, source_target_pairs={{1,0},{2,1},{3,2},{4,3},{5,4},{6,5},{7,6},{8,7},{9,8},{10,9},{11,1... | collective-permute-start | bytes 262088 | tf_op jit(solution)/shard_map/ppermute | solution.py:51
  69.0 7.4 %collective-permute-start.8 = (f32[21,8,8,1]{0,2,3,1:T(8,128)S(1)}, f32[21,8,8,1]{0,2,3,1:T(8,128)S(1)}, u32[]{:S(2)}, u32[]{:S(2)}) collective-permute-start(f32[21,8,8,1]{0,2,3,1:T(8,128)S(1)} %copy.40), channel_id=1, source_target_pairs={{0,16},{16,32},{32,48},{48,64},{64,80},{80,96},{96,112},{112,128},... | collective-permute-start | bytes 16136 | tf_op jit(solution)/shard_map/ppermute | solution.py:48
  70.3 6.9 %collective-permute-start.9 = (f32[21,8,8,1]{0,2,3,1:T(8,128)S(1)}, f32[21,8,8,1]{0,2,3,1:T(8,128)S(1)}, u32[]{:S(2)}, u32[]{:S(2)}) collective-permute-start(f32[21,8,8,1]{0,2,3,1:T(8,128)S(1)} %copy.42), channel_id=1, source_target_pairs={{16,0},{32,16},{48,32},{64,48},{80,64},{96,80},{112,96},{128,112},... | collective-permute-start | bytes 16136 | tf_op jit(solution)/shard_map/ppermute | solution.py:51
  79.3 8.2 %collective-permute-start.10 = (f32[21,8,1,130]{3,2,1,0:T(1,128)S(1)}, f32[21,8,1,130]{3,2,1,0:T(1,128)S(1)}, u32[]{:S(2)}, u32[]{:S(2)}) collective-permute-start(f32[21,8,1,130]{3,2,1,0:T(1,128)S(1)} %get-tuple-element.340), channel_id=1, source_target_pairs={{0,1},{1,2},{2,3},{3,4},{4,5},{5,6},{6,7},{7,8},{8,9},{9,10},{10,1... | collective-permute-start | bytes 262088 | tf_op jit(solution)/shard_map/ppermute | solution.py:48
  79.4 8.2 %collective-permute-start.11 = (f32[21,8,1,130]{3,2,1,0:T(1,128)S(1)}, f32[21,8,1,130]{3,2,1,0:T(1,128)S(1)}, u32[]{:S(2)}, u32[]{:S(2)}) collective-permute-start(f32[21,8,1,130]{3,2,1,0:T(1,128)S(1)} %get-tuple-element.341), channel_id=1, source_target_pairs={{1,0},{2,1},{3,2},{4,3},{5,4},{6,5},{7,6},{8,7},{9,8},{10,9},{11,1... | collective-permute-start | bytes 262088 | tf_op jit(solution)/shard_map/ppermute | solution.py:51
  104.7 7.4 %collective-permute-start.12 = (f32[21,8,8,1]{0,2,3,1:T(8,128)S(1)}, f32[21,8,8,1]{0,2,3,1:T(8,128)S(1)}, u32[]{:S(2)}, u32[]{:S(2)}) collective-permute-start(f32[21,8,8,1]{0,2,3,1:T(8,128)S(1)} %copy.46), channel_id=1, source_target_pairs={{0,16},{16,32},{32,48},{48,64},{64,80},{80,96},{96,112},{112,128},... | collective-permute-start | bytes 16136 | tf_op jit(solution)/shard_map/ppermute | solution.py:48
  106.0 6.9 %collective-permute-start.13 = (f32[21,8,8,1]{0,2,3,1:T(8,128)S(1)}, f32[21,8,8,1]{0,2,3,1:T(8,128)S(1)}, u32[]{:S(2)}, u32[]{:S(2)}) collective-permute-start(f32[21,8,8,1]{0,2,3,1:T(8,128)S(1)} %copy.48), channel_id=1, source_target_pairs={{16,0},{32,16},{48,32},{64,48},{80,64},{96,80},{112,96},{128,112},... | collective-permute-start | bytes 16136 | tf_op jit(solution)/shard_map/ppermute | solution.py:51
  115.0 8.4 %collective-permute-start.14 = (f32[21,8,1,130]{3,2,1,0:T(1,128)S(1)}, f32[21,8,1,130]{3,2,1,0:T(1,128)S(1)}, u32[]{:S(2)}, u32[]{:S(2)}) collective-permute-start(f32[21,8,1,130]{3,2,1,0:T(1,128)S(1)} %get-tuple-element.334), channel_id=1, source_target_pairs={{0,1},{1,2},{2,3},{3,4},{4,5},{5,6},{6,7},{7,8},{8,9},{9,10},{10,1... | collective-permute-start | bytes 262088 | tf_op jit(solution)/shard_map/ppermute | solution.py:48
  115.1 8.3 %collective-permute-start.15 = (f32[21,8,1,130]{3,2,1,0:T(1,128)S(1)}, f32[21,8,1,130]{3,2,1,0:T(1,128)S(1)}, u32[]{:S(2)}, u32[]{:S(2)}) collective-permute-start(f32[21,8,1,130]{3,2,1,0:T(1,128)S(1)} %get-tuple-element.335), channel_id=1, source_target_pairs={{1,0},{2,1},{3,2},{4,3},{5,4},{6,5},{7,6},{8,7},{9,8},{10,9},{11,1... | collective-permute-start | bytes 262088 | tf_op jit(solution)/shard_map/ppermute | solution.py:51
  140.2 13.3 %collective-permute-start.16 = (f32[21,8,8,1]{0,2,3,1:T(8,128)S(1)}, f32[21,8,8,1]{0,2,3,1:T(8,128)S(1)}, u32[]{:S(2)}, u32[]{:S(2)}) collective-permute-start(f32[21,8,8,1]{0,2,3,1:T(8,128)S(1)} %copy.52), channel_id=1, source_target_pairs={{0,16},{16,32},{32,48},{48,64},{64,80},{80,96},{96,112},{112,128},... | collective-permute-start | bytes 16136 | tf_op jit(solution)/shard_map/ppermute | solution.py:48
  141.4 12.8 %collective-permute-start.17 = (f32[21,8,8,1]{0,2,3,1:T(8,128)S(1)}, f32[21,8,8,1]{0,2,3,1:T(8,128)S(1)}, u32[]{:S(2)}, u32[]{:S(2)}) collective-permute-start(f32[21,8,8,1]{0,2,3,1:T(8,128)S(1)} %copy.54), channel_id=1, source_target_pairs={{16,0},{32,16},{48,32},{64,48},{80,64},{96,80},{112,96},{128,112},... | collective-permute-start | bytes 16136 | tf_op jit(solution)/shard_map/ppermute | solution.py:51
  146.2 21.8 %collective-permute-start.22 = (f32[1,8,1,130]{3,2,1,0:T(1,128)}, f32[1,8,1,130]{3,2,1,0:T(1,128)}, u32[]{:S(2)}, u32[]{:S(2)}) collective-permute-start(f32[1,8,1,130]{3,2,1,0:T(1,128)} %get-tuple-element.428), channel_id=1, source_target_pairs={{1,0},{2,1},{3,2},{4,3},{5,4},{6,5},{7,6},{8,7},{9,8},{10,9},{11,1... | collective-permute-start | bytes 12488 | tf_op jit(solution)/shard_map/ppermute | solution.py:51
  151.3 16.7 %collective-permute-start.23 = (f32[1,8,1,130]{3,2,1,0:T(1,128)}, f32[1,8,1,130]{3,2,1,0:T(1,128)}, u32[]{:S(2)}, u32[]{:S(2)}) collective-permute-start(f32[1,8,1,130]{3,2,1,0:T(1,128)} %get-tuple-element.429), channel_id=1, source_target_pairs={{0,1},{1,2},{2,3},{3,4},{4,5},{5,6},{6,7},{7,8},{8,9},{9,10},{10,1... | collective-permute-start | bytes 12488 | tf_op jit(solution)/shard_map/ppermute | solution.py:48
  156.4 7.7 %collective-permute-start.18 = (f32[21,8,1,130]{3,2,1,0:T(1,128)S(1)}, f32[21,8,1,130]{3,2,1,0:T(1,128)S(1)}, u32[]{:S(2)}, u32[]{:S(2)}) collective-permute-start(f32[21,8,1,130]{3,2,1,0:T(1,128)S(1)} %get-tuple-element.329), channel_id=1, source_target_pairs={{0,1},{1,2},{2,3},{3,4},{4,5},{5,6},{6,7},{7,8},{8,9},{9,10},{10,1... | collective-permute-start | bytes 262088 | tf_op jit(solution)/shard_map/ppermute | solution.py:48
  156.5 7.6 %collective-permute-start.19 = (f32[21,8,1,130]{3,2,1,0:T(1,128)S(1)}, f32[21,8,1,130]{3,2,1,0:T(1,128)S(1)}, u32[]{:S(2)}, u32[]{:S(2)}) collective-permute-start(f32[21,8,1,130]{3,2,1,0:T(1,128)S(1)} %get-tuple-element.328), channel_id=1, source_target_pairs={{1,0},{2,1},{3,2},{4,3},{5,4},{6,5},{7,6},{8,7},{9,8},{10,9},{11,1... | collective-permute-start | bytes 262088 | tf_op jit(solution)/shard_map/ppermute | solution.py:51
  169.9 14.1 %collective-permute-start.24 = (f32[2,8,8,1]{3,0,2,1:T(2,128)S(1)}, f32[2,8,8,1]{3,0,2,1:T(2,128)S(1)}, u32[]{:S(2)}, u32[]{:S(2)}) collective-permute-start(f32[2,8,8,1]{3,0,2,1:T(2,128)S(1)} %get-tuple-element.502), channel_id=1, source_target_pairs={{0,16},{16,32},{32,48},{48,64},{64,80},{80,96},{96,112},{112,128},... | collective-permute-start | bytes 1544 | tf_op jit(solution)/shard_map/ppermute | solution.py:48
  170.7 13.3 %collective-permute-start.25 = (f32[2,8,8,1]{3,0,2,1:T(2,128)S(1)}, f32[2,8,8,1]{3,0,2,1:T(2,128)S(1)}, u32[]{:S(2)}, u32[]{:S(2)}) collective-permute-start(f32[2,8,8,1]{3,0,2,1:T(2,128)S(1)} %get-tuple-element.501), channel_id=1, source_target_pairs={{16,0},{32,16},{48,32},{64,48},{80,64},{96,80},{112,96},{128,112},... | collective-permute-start | bytes 1544 | tf_op jit(solution)/shard_map/ppermute | solution.py:51
  184.2 6.1 %collective-permute-start.26 = (f32[2,8,1,130]{3,0,2,1:T(2,128)S(1)}, f32[2,8,1,130]{3,0,2,1:T(2,128)S(1)}, u32[]{:S(2)}, u32[]{:S(2)}) collective-permute-start(f32[2,8,1,130]{3,0,2,1:T(2,128)S(1)} %get-tuple-element.402), channel_id=1, source_target_pairs={{1,0},{2,1},{3,2},{4,3},{5,4},{6,5},{7,6},{8,7},{9,8},{10,9},{11,1... | collective-permute-start | bytes 24968 | tf_op jit(solution)/shard_map/ppermute | solution.py:51
  189.5 5.9 %collective-permute-start.27 = (f32[2,8,1,130]{3,0,2,1:T(2,128)S(1)}, f32[2,8,1,130]{3,0,2,1:T(2,128)S(1)}, u32[]{:S(2)}, u32[]{:S(2)}) collective-permute-start(f32[2,8,1,130]{3,0,2,1:T(2,128)S(1)} %get-tuple-element.403), channel_id=1, source_target_pairs={{0,1},{1,2},{2,3},{3,4},{4,5},{5,6},{6,7},{7,8},{8,9},{9,10},{10,1... | collective-permute-start | bytes 24968 | tf_op jit(solution)/shard_map/ppermute | solution.py:48
  201.6 6.0 %collective-permute-start.31 = (f32[2,8,1,130]{3,0,2,1:T(2,128)S(1)}, f32[2,8,1,130]{3,0,2,1:T(2,128)S(1)}, u32[]{:S(2)}, u32[]{:S(2)}) collective-permute-start(f32[2,8,1,130]{3,0,2,1:T(2,128)S(1)} %get-tuple-element.399), channel_id=1, source_target_pairs={{0,1},{1,2},{2,3},{3,4},{4,5},{5,6},{6,7},{7,8},{8,9},{9,10},{10,1... | collective-permute-start | bytes 24968 | tf_op jit(solution)/shard_map/ppermute | solution.py:48
  208.2 6.0 %collective-permute-start.33 = (f32[2,8,8,1]{3,0,2,1:T(2,128)S(1)}, f32[2,8,8,1]{3,0,2,1:T(2,128)S(1)}, u32[]{:S(2)}, u32[]{:S(2)}) collective-permute-start(f32[2,8,8,1]{3,0,2,1:T(2,128)S(1)} %get-tuple-element.487), channel_id=1, source_target_pairs={{16,0},{32,16},{48,32},{64,48},{80,64},{96,80},{112,96},{128,112},... | collective-permute-start | bytes 1544 | tf_op jit(solution)/shard_map/ppermute | solution.py:51
  214.4 6.2 %collective-permute-start.35 = (f32[2,8,1,130]{3,0,2,1:T(2,128)S(1)}, f32[2,8,1,130]{3,0,2,1:T(2,128)S(1)}, u32[]{:S(2)}, u32[]{:S(2)}) collective-permute-start(f32[2,8,1,130]{3,0,2,1:T(2,128)S(1)} %get-tuple-element.397), channel_id=1, source_target_pairs={{0,1},{1,2},{2,3},{3,4},{4,5},{5,6},{6,7},{7,8},{8,9},{9,10},{10,1... | collective-permute-start | bytes 24968 | tf_op jit(solution)/shard_map/ppermute | solution.py:48
  221.3 6.0 %collective-permute-start.37 = (f32[1,8,8,1]{3,0,2,1:T(1,128)S(1)}, f32[1,8,8,1]{3,0,2,1:T(1,128)S(1)}, u32[]{:S(2)}, u32[]{:S(2)}) collective-permute-start(f32[1,8,8,1]{3,0,2,1:T(1,128)S(1)} %get-tuple-element.481), channel_id=1, source_target_pairs={{16,0},{32,16},{48,32},{64,48},{80,64},{96,80},{112,96},{128,112},... | collective-permute-start | bytes 776 | tf_op jit(solution)/shard_map/ppermute | solution.py:51
  336.2 6.0 %collective-permute-start.47 = (f32[2,8,1,130]{3,0,2,1:T(2,128)S(1)}, f32[2,8,1,130]{3,0,2,1:T(2,128)S(1)}, u32[]{:S(2)}, u32[]{:S(2)}) collective-permute-start(f32[2,8,1,130]{3,0,2,1:T(2,128)S(1)} %get-tuple-element.393), channel_id=1, source_target_pairs={{0,1},{1,2},{2,3},{3,4},{4,5},{5,6},{6,7},{7,8},{8,9},{9,10},{10,1... | collective-permute-start | bytes 24968 | tf_op jit(solution)/shard_map/ppermute | solution.py:48
  348.2 6.2 %collective-permute-start.51 = (f32[2,8,1,130]{3,0,2,1:T(2,128)S(1)}, f32[2,8,1,130]{3,0,2,1:T(2,128)S(1)}, u32[]{:S(2)}, u32[]{:S(2)}) collective-permute-start(f32[2,8,1,130]{3,0,2,1:T(2,128)S(1)} %get-tuple-element.391), channel_id=1, source_target_pairs={{0,1},{1,2},{2,3},{3,4},{4,5},{5,6},{6,7},{7,8},{8,9},{9,10},{10,1... | collective-permute-start | bytes 24968 | tf_op jit(solution)/shard_map/ppermute | solution.py:48
  (299 other events, 704.9 us)
